TPU v7x, 256 devices: a whole 4x4x8 slice. The times are simulated.
256 devices in a mesh: ctx: 16 (over z, core), head: 16 (over x, y).
Axes of the slice: x: 4, y: 4, z: 8, core: 2. Of those that a mesh axis runs over, the one named last changes fastest.
Arguments:
- queries: float32 [24576, 16, 4, 128], P(('ctx', 'head')), may hold values from -6 to 6
- key_vectors: float32 [24576, 16, 4, 128], P(('ctx', 'head')), may hold values from -0.6 to 0.6
- value_vectors: float32 [24576, 16, 4, 128], P(('ctx', 'head')), may hold values from -6 to 6
- log_decay: float32 [24576, 16, 4], P(('ctx', 'head')), may hold values from -1.5 to 0
- doc_lengths: int32 [16], replicated, may hold values from 1 to 6144, 24576 in all
Outputs:
- lightning_out: float32 [24576, 64, 128], P('ctx', 'head')
Inputs may be any that keep to these rules, and one draw needn't show every extreme that they name: `doc_lengths`: the 16 documents lie end to end and fill all 24576 tokens; the longest has exactly 6144 tokens.
All inputs are finite; a program needn't handle non-finite values.
Results may differ from a plain program's by a relative error of at most 0.0003.
Values sent between devices are 32-bit elements; how exact they have to be, the bound alone decides.
A program may use at most 128 MiB of HBM per device.

v0:
```python
from functools import partial

import jax
import jax.numpy as jnp
from jax import lax
from jax.sharding import PartitionSpec as P

PRECISE = lax.Precision.HIGHEST
EPSILON = 1e-06


def from_behind(block, axis, distance):
    devices = range(lax.axis_size(axis))
    route = [(i - distance, i) for i in devices if i - distance in devices]
    return lax.ppermute(block, axis, route)


def block_step(carry_in, block_in, want_out):
    state, factor = carry_in
    query_rows, key_rows, value_rows, gate_rows, doc_ids, prev_doc = block_in
    block_len = doc_ids.shape[0]
    cumulative = jnp.cumsum(gate_rows, axis=0)
    row_index = lax.broadcasted_iota(jnp.int32, (block_len, block_len), 0)
    col_index = lax.broadcasted_iota(jnp.int32, (block_len, block_len), 1)
    visible = (row_index >= col_index) & (doc_ids[:, None] == doc_ids[None, :])
    heads_cum = jnp.transpose(cumulative)
    exponent = heads_cum[:, :, None] - heads_cum[:, None, :]
    weights = jnp.where(visible[None], jnp.exp(jnp.where(visible[None], exponent, 0.0)), 0.0)
    carry_coef = jnp.where((doc_ids == prev_doc)[:, None], jnp.exp(cumulative), 0.0)
    tail_coef = jnp.where(
        (doc_ids == doc_ids[block_len - 1])[:, None],
        jnp.exp(cumulative[block_len - 1][None, :] - cumulative),
        0.0,
    )
    new_state = (
        jnp.einsum("shd,she->hde", key_rows * tail_coef[:, :, None], value_rows, precision=PRECISE)
        + carry_coef[block_len - 1][:, None, None] * state
    )
    new_factor = carry_coef[block_len - 1] * factor
    scores = jnp.einsum("thd,shd->hts", query_rows, key_rows, precision=PRECISE) * weights
    local_out = jnp.einsum("hts,shd->thd", scores, value_rows, precision=PRECISE)
    carried = jnp.einsum("thd,hde->the", query_rows, state, precision=PRECISE)
    return (
        (new_state, new_factor),
        (local_out + carry_coef[:, :, None] * carried, carry_coef * factor[None, :]),
    )


def chain_in(factor, local_state):

    def turn(step, incoming):
        outgoing = factor[:, None, None] * incoming + local_state
        return from_behind(outgoing, "ctx", 1)

    return lax.fori_loop(0, lax.axis_size("ctx") - 1, turn, jnp.zeros_like(local_state))


def lightning_rows(query_rows, key_rows, value_rows, gate_rows, doc_lengths):
    query_rows = query_rows[:, 0]
    key_rows = key_rows[:, 0]
    value_rows = value_rows[:, 0]
    gate_rows = gate_rows[:, 0]
    tok_count, head_count, head_dim = query_rows.shape
    block_len = min(512, tok_count)
    block_count = tok_count // block_len
    first_pos = lax.axis_index("ctx") * tok_count
    positions = first_pos + lax.iota(jnp.int32, tok_count)
    doc_ends = jnp.cumsum(doc_lengths)
    doc_ids = jnp.sum((doc_ends[None, :] <= positions[:, None]).astype(jnp.int32), axis=1)
    before_doc = jnp.sum((doc_ends <= first_pos - 1).astype(jnp.int32))
    before_doc = jnp.where(first_pos > 0, before_doc, -1)
    block_docs = doc_ids.reshape(block_count, block_len)
    prev_docs = jnp.concatenate([before_doc[None], block_docs[:-1, block_len - 1]])
    blocked = (
        query_rows.reshape(block_count, block_len, head_count, head_dim),
        key_rows.reshape(block_count, block_len, head_count, head_dim),
        value_rows.reshape(block_count, block_len, head_count, head_dim),
        gate_rows.reshape(block_count, block_len, head_count),
        block_docs,
        prev_docs,
    )
    empty_state = jnp.zeros((head_count, head_dim, head_dim), jnp.float32)
    start_carry = (empty_state, jnp.ones((head_count,), jnp.float32))
    final_carry, outputs = lax.scan(partial(block_step, want_out=True), start_carry, blocked)
    incoming = chain_in(final_carry[1], final_carry[0])
    coefficients = outputs[1]
    mixed_rows = outputs[0] + coefficients[..., None] * jnp.einsum(
        "bthd,hde->bthe", blocked[0], incoming, precision=PRECISE
    )
    mixed_rows = mixed_rows.reshape(tok_count, head_count, head_dim)
    return mixed_rows * lax.rsqrt(
        jnp.mean(mixed_rows * mixed_rows, axis=-1, keepdims=True) + EPSILON
    )


def per_device(queries, key_vectors, value_vectors, log_decay, doc_lengths):
    return lightning_rows(
        lax.all_to_all(queries, "head", split_axis=1, concat_axis=0, tiled=True),
        lax.all_to_all(key_vectors, "head", split_axis=1, concat_axis=0, tiled=True),
        lax.all_to_all(value_vectors, "head", split_axis=1, concat_axis=0, tiled=True),
        lax.all_to_all(log_decay, "head", split_axis=1, concat_axis=0, tiled=True),
        doc_lengths,
    )


def solution(mesh):
    return jax.shard_map(
        per_device,
        mesh=mesh,
        in_specs=(
            P(("ctx", "head"), None, None, None),
            P(("ctx", "head"), None, None, None),
            P(("ctx", "head"), None, None, None),
            P(("ctx", "head"), None, None),
            P(),
        ),
        out_specs=P("ctx", "head", None),
        check_vma=False,
    )
```

profile of v0, /device:TPU:128, one launch (start us, length us, event | category | flops | bytes accessed | tf_op | source)
XLA Modules:
  0.0 442.2 jit_solution(5141908334843948772)
XLA Ops:
  24.0 38.2 %all-to-all-done = f32[96,16,4,128]{3,0,2,1:T(8,128)S(1)} async-done(((f32[96,16,4,128]{3,0,2,1:T(8,128)}), f32[96,16,4,128]{3,0,2,1:T(8,128)S(1)}, u32[]{:S(2)}, u32[]{:S(2)}) %all-to-all-start) | async-done | bytes 3145760 | tf_op jit(solution)/shard_map/all_to_all | solution.py:99
  73.8 32.8 %all-to-all-done.3 = f32[96,16,4,128]{3,2,0,1:T(4,128)} async-done(((f32[96,16,4,128]{3,2,0,1:T(4,128)}), f32[96,16,4,128]{3,2,0,1:T(4,128)}, u32[]{:S(2)}, u32[]{:S(2)}) %all-to-all-start.3) | async-done | bytes 3145760 | tf_op jit(solution)/shard_map/all_to_all | solution.py:98
  118.5 34.4 %all-to-all-done.2 = f32[96,16,4,128]{3,0,2,1:T(8,128)} async-done(((f32[96,16,4,128]{3,0,2,1:T(8,128)}), f32[96,16,4,128]{3,0,2,1:T(8,128)}, u32[]{:S(2)}, u32[]{:S(2)}) %all-to-all-start.2) | async-done | bytes 3145760 | tf_op jit(solution)/shard_map/all_to_all | solution.py:100
  156.8 102.6 %while.28 = (s32[]{:T(128)}, f32[4,128,128]{2,1,0:T(8,128)S(1)}, f32[4]{0:T(128)S(1)}, f32[3,512,4,128]{1,3,0,2:T(8,128)}, f32[3,512,4]{1,0,2:T(4,128)S(1)}, /*i...) while((s32[]{:T(128)}, f32[4,128,128]{2,1,0:T(8,128)S(1)}, ...), condition=%wide.region_6.7_spmd.clone, body=%wide.region_3.6_spmd.clone.sunk | while | flops 4032832512 | bytes 19397364 | solution.py:84
  165.0 8.3 %fusion.67 = f32[512,4,128]{0,2,1:T(8,128)} fusion(f32[4,512,512]{2,1,0:T(8,128)} %fusion.65, f32[4,512]{1,0:T(4,128)S(1)} %bitcast.155, pred[512,512]{1,0:T(8,128)(4,1)S(1)} %fusion.66, f32[3,512,4,128]{3,1,0,2:T(8,128)} %get-tuple-element.360, s32[]{:T(128)S(6)} %copy.142), kind=kOutput, calls=%fused_computation.11.clone.1 | convolution fusion | flops 1614807040 | bytes 6569988 | tf_op jit(solution)/shard_map/while/body/eval_jaxpr/hts,shd->thd/dot_general | solution.py:41
  199.2 8.3 %fusion.67 = f32[512,4,128]{0,2,1:T(8,128)} fusion(f32[4,512,512]{2,1,0:T(8,128)} %fusion.65, f32[4,512]{1,0:T(4,128)S(1)} %bitcast.155, pred[512,512]{1,0:T(8,128)(4,1)S(1)} %fusion.66, f32[3,512,4,128]{3,1,0,2:T(8,128)} %get-tuple-element.360, s32[]{:T(128)S(6)} %copy.142), kind=kOutput, calls=%fused_computation.11.clone.1 | convolution fusion | flops 1614807040 | bytes 6569988 | tf_op jit(solution)/shard_map/while/body/eval_jaxpr/hts,shd->thd/dot_general | solution.py:41
  233.4 8.3 %fusion.67 = f32[512,4,128]{0,2,1:T(8,128)} fusion(f32[4,512,512]{2,1,0:T(8,128)} %fusion.65, f32[4,512]{1,0:T(4,128)S(1)} %bitcast.155, pred[512,512]{1,0:T(8,128)(4,1)S(1)} %fusion.66, f32[3,512,4,128]{3,1,0,2:T(8,128)} %get-tuple-element.360, s32[]{:T(128)S(6)} %copy.142), kind=kOutput, calls=%fused_computation.11.clone.1 | convolution fusion | flops 1614807040 | bytes 6569988 | tf_op jit(solution)/shard_map/while/body/eval_jaxpr/hts,shd->thd/dot_general | solution.py:41
  260.1 164.1 %while.27 = (s32[]{:T(128)}, f32[4,128,128]{2,1,0:T(8,128)}, f32[4]{0:T(128)S(1)}, f32[4,128,128]{2,1,0:T(8,128)S(1)}, s32[]{:T(128)}) while((s32[]{:T(128)}, f32[4,128,128]{2,1,0:T(8,128)}, f32[4]{0:T(128)S(1)}, f32[4,128,128]{2,1,0:T(8,128)S(1)}, s32[]{:T(128)}) %tuple.51), condition=%wide.region_8.9_spmd, body=%wide.region_7.8_spmd.sunk | while | flops 131074 | bytes 1835125 | solution.py:55
  263.7 7.3 %collective-permute-done = f32[4,128,128]{2,1,0:T(8,128)} collective-permute-done((f32[4,128,128]{2,1,0:T(8,128)}, f32[4,128,128]{2,1,0:T(8,128)}, u32[]{:S(2)}, u32[]{:S(2)}) %collective-permute-start) | collective-permute-done | bytes 262176 | tf_op jit(solution)/shard_map/while/body/eval_jaxpr/ppermute | solution.py:15
  274.7 7.3 %collective-permute-done = f32[4,128,128]{2,1,0:T(8,128)} collective-permute-done((f32[4,128,128]{2,1,0:T(8,128)}, f32[4,128,128]{2,1,0:T(8,128)}, u32[]{:S(2)}, u32[]{:S(2)}) %collective-permute-start) | collective-permute-done | bytes 262176 | tf_op jit(solution)/shard_map/while/body/eval_jaxpr/ppermute | solution.py:15
  285.6 7.3 %collective-permute-done = f32[4,128,128]{2,1,0:T(8,128)} collective-permute-done((f32[4,128,128]{2,1,0:T(8,128)}, f32[4,128,128]{2,1,0:T(8,128)}, u32[]{:S(2)}, u32[]{:S(2)}) %collective-permute-start) | collective-permute-done | bytes 262176 | tf_op jit(solution)/shard_map/while/body/eval_jaxpr/ppermute | solution.py:15
  296.6 7.3 %collective-permute-done = f32[4,128,128]{2,1,0:T(8,128)} collective-permute-done((f32[4,128,128]{2,1,0:T(8,128)}, f32[4,128,128]{2,1,0:T(8,128)}, u32[]{:S(2)}, u32[]{:S(2)}) %collective-permute-start) | collective-permute-done | bytes 262176 | tf_op jit(solution)/shard_map/while/body/eval_jaxpr/ppermute | solution.py:15
  307.5 7.3 %collective-permute-done = f32[4,128,128]{2,1,0:T(8,128)} collective-permute-done((f32[4,128,128]{2,1,0:T(8,128)}, f32[4,128,128]{2,1,0:T(8,128)}, u32[]{:S(2)}, u32[]{:S(2)}) %collective-permute-start) | collective-permute-done | bytes 262176 | tf_op jit(solution)/shard_map/while/body/eval_jaxpr/ppermute | solution.py:15
  318.5 7.3 %collective-permute-done = f32[4,128,128]{2,1,0:T(8,128)} collective-permute-done((f32[4,128,128]{2,1,0:T(8,128)}, f32[4,128,128]{2,1,0:T(8,128)}, u32[]{:S(2)}, u32[]{:S(2)}) %collective-permute-start) | collective-permute-done | bytes 262176 | tf_op jit(solution)/shard_map/while/body/eval_jaxpr/ppermute | solution.py:15
  329.4 7.3 %collective-permute-done = f32[4,128,128]{2,1,0:T(8,128)} collective-permute-done((f32[4,128,128]{2,1,0:T(8,128)}, f32[4,128,128]{2,1,0:T(8,128)}, u32[]{:S(2)}, u32[]{:S(2)}) %collective-permute-start) | collective-permute-done | bytes 262176 | tf_op jit(solution)/shard_map/while/body/eval_jaxpr/ppermute | solution.py:15
  340.3 7.3 %collective-permute-done = f32[4,128,128]{2,1,0:T(8,128)} collective-permute-done((f32[4,128,128]{2,1,0:T(8,128)}, f32[4,128,128]{2,1,0:T(8,128)}, u32[]{:S(2)}, u32[]{:S(2)}) %collective-permute-start) | collective-permute-done | bytes 262176 | tf_op jit(solution)/shard_map/while/body/eval_jaxpr/ppermute | solution.py:15
  351.3 7.3 %collective-permute-done = f32[4,128,128]{2,1,0:T(8,128)} collective-permute-done((f32[4,128,128]{2,1,0:T(8,128)}, f32[4,128,128]{2,1,0:T(8,128)}, u32[]{:S(2)}, u32[]{:S(2)}) %collective-permute-start) | collective-permute-done | bytes 262176 | tf_op jit(solution)/shard_map/while/body/eval_jaxpr/ppermute | solution.py:15
  362.2 7.3 %collective-permute-done = f32[4,128,128]{2,1,0:T(8,128)} collective-permute-done((f32[4,128,128]{2,1,0:T(8,128)}, f32[4,128,128]{2,1,0:T(8,128)}, u32[]{:S(2)}, u32[]{:S(2)}) %collective-permute-start) | collective-permute-done | bytes 262176 | tf_op jit(solution)/shard_map/while/body/eval_jaxpr/ppermute | solution.py:15
  373.2 7.3 %collective-permute-done = f32[4,128,128]{2,1,0:T(8,128)} collective-permute-done((f32[4,128,128]{2,1,0:T(8,128)}, f32[4,128,128]{2,1,0:T(8,128)}, u32[]{:S(2)}, u32[]{:S(2)}) %collective-permute-start) | collective-permute-done | bytes 262176 | tf_op jit(solution)/shard_map/while/body/eval_jaxpr/ppermute | solution.py:15
  384.1 7.3 %collective-permute-done = f32[4,128,128]{2,1,0:T(8,128)} collective-permute-done((f32[4,128,128]{2,1,0:T(8,128)}, f32[4,128,128]{2,1,0:T(8,128)}, u32[]{:S(2)}, u32[]{:S(2)}) %collective-permute-start) | collective-permute-done | bytes 262176 | tf_op jit(solution)/shard_map/while/body/eval_jaxpr/ppermute | solution.py:15
  395.1 7.3 %collective-permute-done = f32[4,128,128]{2,1,0:T(8,128)} collective-permute-done((f32[4,128,128]{2,1,0:T(8,128)}, f32[4,128,128]{2,1,0:T(8,128)}, u32[]{:S(2)}, u32[]{:S(2)}) %collective-permute-start) | collective-permute-done | bytes 262176 | tf_op jit(solution)/shard_map/while/body/eval_jaxpr/ppermute | solution.py:15
  406.0 7.3 %collective-permute-done = f32[4,128,128]{2,1,0:T(8,128)} collective-permute-done((f32[4,128,128]{2,1,0:T(8,128)}, f32[4,128,128]{2,1,0:T(8,128)}, u32[]{:S(2)}, u32[]{:S(2)}) %collective-permute-start) | collective-permute-done | bytes 262176 | tf_op jit(solution)/shard_map/while/body/eval_jaxpr/ppermute | solution.py:15
  416.9 7.3 %collective-permute-done = f32[4,128,128]{2,1,0:T(8,128)} collective-permute-done((f32[4,128,128]{2,1,0:T(8,128)}, f32[4,128,128]{2,1,0:T(8,128)}, u32[]{:S(2)}, u32[]{:S(2)}) %collective-permute-start) | collective-permute-done | bytes 262176 | tf_op jit(solution)/shard_map/while/body/eval_jaxpr/ppermute | solution.py:15
  434.5 7.7 %copy.101 = f32[1536,4,128]{2,1,0:T(4,128)} copy(f32[1536,4,128]{2,0,1:T(8,128)S(1)} %bitcast_multiply_fusion.2) | data formatting | bytes 6291456 | tf_op jit(solution)/shard_map/mul | solution.py:91
  (146 shorter events, 193.7 us)
Async XLA Ops:
  0.0 14.7 %all-to-all-start.1 = ((f32[96,16,4]{0,2,1:T(4,128)}), f32[96,16,4]{0,2,1:T(4,128)S(1)}, u32[]{:S(2)}, u32[]{:S(2)}) async-start(f32[96,16,4]{0,2,1:T(4,128)} %param.12), calls=%async_computation.1 | async-start | bytes 65536 | tf_op jit(solution)/shard_map/all_to_all | solution.py:101
  14.7 47.6 %all-to-all-start = ((f32[96,16,4,128]{3,0,2,1:T(8,128)}), f32[96,16,4,128]{3,0,2,1:T(8,128)S(1)}, u32[]{:S(2)}, u32[]{:S(2)}) async-start(f32[96,16,4,128]{3,0,2,1:T(8,128)} %copy.85), calls=%async_computation | async-start | bytes 6291456 | tf_op jit(solution)/shard_map/all_to_all | solution.py:99
  62.2 1.7 copy-start
  63.9 42.7 %all-to-all-start.3 = ((f32[96,16,4,128]{3,2,0,1:T(4,128)}), f32[96,16,4,128]{3,2,0,1:T(4,128)}, u32[]{:S(2)}, u32[]{:S(2)}) async-start(f32[96,16,4,128]{3,2,0,1:T(4,128)} %copy.91), calls=%async_computation.3 | async-start | bytes 6291456 | tf_op jit(solution)/shard_map/all_to_all | solution.py:98
  73.8 38.0 %copy-start.2 = (s32[16]{0:T(128)S(1)}, s32[16]{0:T(128)}, u32[]{:S(2)}) copy-start(s32[16]{0:T(128)} %param.13) | copy-start | bytes 196
  106.6 46.4 %all-to-all-start.2 = ((f32[96,16,4,128]{3,0,2,1:T(8,128)}), f32[96,16,4,128]{3,0,2,1:T(8,128)}, u32[]{:S(2)}, u32[]{:S(2)}) async-start(f32[96,16,4,128]{3,0,2,1:T(8,128)} %copy.89), calls=%async_computation.2 | async-start | bytes 6291456 | tf_op jit(solution)/shard_map/all_to_all | solution.py:100
  113.8 2.8 copy-start.1
  261.8 9.2 %collective-permute-start = (f32[4,128,128]{2,1,0:T(8,128)}, f32[4,128,128]{2,1,0:T(8,128)}, u32[]{:S(2)}, u32[]{:S(2)}) collective-permute-start(f32[4,128,128]{2,1,0:T(8,128)} %multiply_add_fusion.2), channel_id=1, source_target_pairs={{0,16},{16,32},{32,48},{48,64},{64,80},{80,96},{96,112},{112,128},... | collective-permute-start | bytes 786440 | tf_op jit(solution)/shard_map/while/body/eval_jaxpr/ppermute | solution.py:15
  272.8 9.2 %collective-permute-start = (f32[4,128,128]{2,1,0:T(8,128)}, f32[4,128,128]{2,1,0:T(8,128)}, u32[]{:S(2)}, u32[]{:S(2)}) collective-permute-start(f32[4,128,128]{2,1,0:T(8,128)} %multiply_add_fusion.2), channel_id=1, source_target_pairs={{0,16},{16,32},{32,48},{48,64},{64,80},{80,96},{96,112},{112,128},... | collective-permute-start | bytes 786440 | tf_op jit(solution)/shard_map/while/body/eval_jaxpr/ppermute | solution.py:15
  283.7 9.2 %collective-permute-start = (f32[4,128,128]{2,1,0:T(8,128)}, f32[4,128,128]{2,1,0:T(8,128)}, u32[]{:S(2)}, u32[]{:S(2)}) collective-permute-start(f32[4,128,128]{2,1,0:T(8,128)} %multiply_add_fusion.2), channel_id=1, source_target_pairs={{0,16},{16,32},{32,48},{48,64},{64,80},{80,96},{96,112},{112,128},... | collective-permute-start | bytes 786440 | tf_op jit(solution)/shard_map/while/body/eval_jaxpr/ppermute | solution.py:15
  294.7 9.2 %collective-permute-start = (f32[4,128,128]{2,1,0:T(8,128)}, f32[4,128,128]{2,1,0:T(8,128)}, u32[]{:S(2)}, u32[]{:S(2)}) collective-permute-start(f32[4,128,128]{2,1,0:T(8,128)} %multiply_add_fusion.2), channel_id=1, source_target_pairs={{0,16},{16,32},{32,48},{48,64},{64,80},{80,96},{96,112},{112,128},... | collective-permute-start | bytes 786440 | tf_op jit(solution)/shard_map/while/body/eval_jaxpr/ppermute | solution.py:15
  305.6 9.2 %collective-permute-start = (f32[4,128,128]{2,1,0:T(8,128)}, f32[4,128,128]{2,1,0:T(8,128)}, u32[]{:S(2)}, u32[]{:S(2)}) collective-permute-start(f32[4,128,128]{2,1,0:T(8,128)} %multiply_add_fusion.2), channel_id=1, source_target_pairs={{0,16},{16,32},{32,48},{48,64},{64,80},{80,96},{96,112},{112,128},... | collective-permute-start | bytes 786440 | tf_op jit(solution)/shard_map/while/body/eval_jaxpr/ppermute | solution.py:15
  316.5 9.2 %collective-permute-start = (f32[4,128,128]{2,1,0:T(8,128)}, f32[4,128,128]{2,1,0:T(8,128)}, u32[]{:S(2)}, u32[]{:S(2)}) collective-permute-start(f32[4,128,128]{2,1,0:T(8,128)} %multiply_add_fusion.2), channel_id=1, source_target_pairs={{0,16},{16,32},{32,48},{48,64},{64,80},{80,96},{96,112},{112,128},... | collective-permute-start | bytes 786440 | tf_op jit(solution)/shard_map/while/body/eval_jaxpr/ppermute | solution.py:15
  327.5 9.2 %collective-permute-start = (f32[4,128,128]{2,1,0:T(8,128)}, f32[4,128,128]{2,1,0:T(8,128)}, u32[]{:S(2)}, u32[]{:S(2)}) collective-permute-start(f32[4,128,128]{2,1,0:T(8,128)} %multiply_add_fusion.2), channel_id=1, source_target_pairs={{0,16},{16,32},{32,48},{48,64},{64,80},{80,96},{96,112},{112,128},... | collective-permute-start | bytes 786440 | tf_op jit(solution)/shard_map/while/body/eval_jaxpr/ppermute | solution.py:15
  338.4 9.2 %collective-permute-start = (f32[4,128,128]{2,1,0:T(8,128)}, f32[4,128,128]{2,1,0:T(8,128)}, u32[]{:S(2)}, u32[]{:S(2)}) collective-permute-start(f32[4,128,128]{2,1,0:T(8,128)} %multiply_add_fusion.2), channel_id=1, source_target_pairs={{0,16},{16,32},{32,48},{48,64},{64,80},{80,96},{96,112},{112,128},... | collective-permute-start | bytes 786440 | tf_op jit(solution)/shard_map/while/body/eval_jaxpr/ppermute | solution.py:15
  349.4 9.2 %collective-permute-start = (f32[4,128,128]{2,1,0:T(8,128)}, f32[4,128,128]{2,1,0:T(8,128)}, u32[]{:S(2)}, u32[]{:S(2)}) collective-permute-start(f32[4,128,128]{2,1,0:T(8,128)} %multiply_add_fusion.2), channel_id=1, source_target_pairs={{0,16},{16,32},{32,48},{48,64},{64,80},{80,96},{96,112},{112,128},... | collective-permute-start | bytes 786440 | tf_op jit(solution)/shard_map/while/body/eval_jaxpr/ppermute | solution.py:15
  360.3 9.2 %collective-permute-start = (f32[4,128,128]{2,1,0:T(8,128)}, f32[4,128,128]{2,1,0:T(8,128)}, u32[]{:S(2)}, u32[]{:S(2)}) collective-permute-start(f32[4,128,128]{2,1,0:T(8,128)} %multiply_add_fusion.2), channel_id=1, source_target_pairs={{0,16},{16,32},{32,48},{48,64},{64,80},{80,96},{96,112},{112,128},... | collective-permute-start | bytes 786440 | tf_op jit(solution)/shard_map/while/body/eval_jaxpr/ppermute | solution.py:15
  371.2 9.2 %collective-permute-start = (f32[4,128,128]{2,1,0:T(8,128)}, f32[4,128,128]{2,1,0:T(8,128)}, u32[]{:S(2)}, u32[]{:S(2)}) collective-permute-start(f32[4,128,128]{2,1,0:T(8,128)} %multiply_add_fusion.2), channel_id=1, source_target_pairs={{0,16},{16,32},{32,48},{48,64},{64,80},{80,96},{96,112},{112,128},... | collective-permute-start | bytes 786440 | tf_op jit(solution)/shard_map/while/body/eval_jaxpr/ppermute | solution.py:15
  382.2 9.2 %collective-permute-start = (f32[4,128,128]{2,1,0:T(8,128)}, f32[4,128,128]{2,1,0:T(8,128)}, u32[]{:S(2)}, u32[]{:S(2)}) collective-permute-start(f32[4,128,128]{2,1,0:T(8,128)} %multiply_add_fusion.2), channel_id=1, source_target_pairs={{0,16},{16,32},{32,48},{48,64},{64,80},{80,96},{96,112},{112,128},... | collective-permute-start | bytes 786440 | tf_op jit(solution)/shard_map/while/body/eval_jaxpr/ppermute | solution.py:15
  393.1 9.2 %collective-permute-start = (f32[4,128,128]{2,1,0:T(8,128)}, f32[4,128,128]{2,1,0:T(8,128)}, u32[]{:S(2)}, u32[]{:S(2)}) collective-permute-start(f32[4,128,128]{2,1,0:T(8,128)} %multiply_add_fusion.2), channel_id=1, source_target_pairs={{0,16},{16,32},{32,48},{48,64},{64,80},{80,96},{96,112},{112,128},... | collective-permute-start | bytes 786440 | tf_op jit(solution)/shard_map/while/body/eval_jaxpr/ppermute | solution.py:15
  404.1 9.2 %collective-permute-start = (f32[4,128,128]{2,1,0:T(8,128)}, f32[4,128,128]{2,1,0:T(8,128)}, u32[]{:S(2)}, u32[]{:S(2)}) collective-permute-start(f32[4,128,128]{2,1,0:T(8,128)} %multiply_add_fusion.2), channel_id=1, source_target_pairs={{0,16},{16,32},{32,48},{48,64},{64,80},{80,96},{96,112},{112,128},... | collective-permute-start | bytes 786440 | tf_op jit(solution)/shard_map/while/body/eval_jaxpr/ppermute | solution.py:15
  415.0 9.2 %collective-permute-start = (f32[4,128,128]{2,1,0:T(8,128)}, f32[4,128,128]{2,1,0:T(8,128)}, u32[]{:S(2)}, u32[]{:S(2)}) collective-permute-start(f32[4,128,128]{2,1,0:T(8,128)} %multiply_add_fusion.2), channel_id=1, source_target_pairs={{0,16},{16,32},{32,48},{48,64},{64,80},{80,96},{96,112},{112,128},... | collective-permute-start | bytes 786440 | tf_op jit(solution)/shard_map/while/body/eval_jaxpr/ppermute | solution.py:15
where the time goes:
time: 445 us; the launch traced here: 442 us
  waiting for transfers between devices  217 us (49%)
  matrix products  71.8 us (16%)
  local copies, waits for them, and re-layouts  57 us (13%)
  starting transfers between devices  50.3 us (11%)
  other arithmetic  44.9 us (10%)
    ppermute x15, waiting for transfers between devices, from_behind(): return lax.ppermute(block, axis, route)  109 us
    all_to_all x1, waiting for transfers between devices, per_device(): lax.all_to_all(key_vectors, 'head', split_axis=1, concat_axis=0, tiled=True)  38.2 us
    all_to_all x1, waiting for transfers between devices, per_device(): lax.all_to_all(value_vectors, 'head', split_axis=1, concat_axis=0, tiled=...  34.4 us
    all_to_all x1, waiting for transfers between devices, per_device(): lax.all_to_all(queries, 'head', split_axis=1, concat_axis=0, tiled=True)  32.8 us
    ppermute x15, starting transfers between devices, from_behind(): return lax.ppermute(block, axis, route)  28.6 us
    add x15, other arithmetic, turn(): outgoing = factor[:, None, None] * incoming + local_state  26 us
    dot_general x3, matrix products, block_step(): jnp.einsum('hts,shd->thd', scores, value_rows, precision=PRECISE)  25 us
    dot_general x3, matrix products, block_step(): jnp.einsum('thd,shd->hts', query_rows, key_rows, precision=PRECISE)  18.8 us
  transfers between devices with their start and end apart: 19, of which 19 were waited for; matrix products, arithmetic and copies ran while one was open for 5% of the time, Pallas kernels for 0%

commit v1 on v0

v1 whole, which is shorter than its diff:
```python
import functools

import jax
import jax.numpy as jnp
from jax import lax
from jax.experimental import pallas as pl
from jax.experimental.pallas import tpu as pltpu
from jax.sharding import PartitionSpec as P

EPSILON = 1e-06
SIDE = 4
BLOCKED = -1e30
EXACT = lax.Precision.HIGHEST
MESH = pl.DeviceIdType.MESH

GROUPS = ((1, 3, 4, 12), (5, 15, 7, 13), (2, 8), (6, 14, 9, 11), (10,))
ORDER = (0,) + sum(GROUPS, ())
FIRST_CODES = sum(off << (4 * n) for n, off in enumerate(ORDER[:8]))
LAST_CODES = sum(off << (4 * n) for n, off in enumerate(ORDER[8:])) - (1 << 32)


def split(x):
    high = x.astype(jnp.bfloat16)
    return high, (x - high.astype(jnp.float32)).astype(jnp.bfloat16)


def twice(high, low):
    row = jnp.concatenate([high, low], axis=1)
    return jnp.concatenate([row, row], axis=0)


def stacked(high, low):
    return jnp.concatenate(
        [jnp.concatenate([high, high], axis=1), jnp.concatenate([low, low], axis=1)],
        axis=0,
    )


def halves(x):
    half = x.shape[1] // 2
    return x[:, :half] + x[:, half:]


def product(left, right):
    return halves(jnp.dot(left, right, preferred_element_type=jnp.float32))


def product_t(left, right):
    return halves(
        lax.dot_general(
            left, right, (((1,), (1,)), ((), ())), preferred_element_type=jnp.float32
        )
    )


def kernel(
    tokens, heads, n_ctx,
    docs, q, k, v, gates, out,
    land, gate_in, keep, tail, carry, step, update,
    k_high, k_low, v_high, v_low, s_high, s_low, own_state, near_states, near_sum, far_sum, rows_out,
    send_sem, recv_sem, gate_send, gate_recv, state_send, state_recv, out_sem,
):
    sources = SIDE * SIDE
    wide = 128
    ctx = lax.axis_index("ctx")
    me = lax.axis_index("head")
    x, y = me // SIDE, me % SIDE

    def to(off):
        return (x + off // SIDE) % SIDE * SIDE + (y + off % SIDE) % SIDE

    def source(n):
        codes = jnp.where(n < 8, FIRST_CODES, LAST_CODES)
        off = lax.shift_right_arithmetic(codes, 4 * (n % 8)) % 16
        return (x + SIDE - off // SIDE) % SIDE * SIDE + (y + SIDE - off % SIDE) % SIDE

    arrays = (k, v, q)
    K, V, Q = range(3)

    for a, array in enumerate(arrays):
        for j in range(heads):
            pltpu.make_async_copy(
                array.at[:, me, j], land.at[a, me, j], recv_sem.at[a, me]
            ).start()
    pltpu.make_async_copy(gates.at[me], gate_in.at[me], gate_recv.at[me]).start()

    barrier = pltpu.get_barrier_semaphore()
    for off in range(1, sources):
        pl.semaphore_signal(barrier, inc=1, device_id={"head": to(off)}, device_id_type=MESH)
    for hop in (1, 2, n_ctx - 1, n_ctx - 2):
        pl.semaphore_signal(
            barrier, inc=1, device_id={"ctx": (ctx + hop) % n_ctx}, device_id_type=MESH
        )
    pl.semaphore_wait(barrier, sources + 3)

    for off in ORDER[1:]:
        pltpu.make_async_remote_copy(
            src_ref=gates.at[to(off)], dst_ref=gate_in.at[me],
            send_sem=gate_send, recv_sem=gate_recv.at[me],
            device_id={"head": to(off)}, device_id_type=MESH,
        ).start()
    for a, array in enumerate(arrays):
        for group in GROUPS:
            for j in range(heads):
                for off in group:
                    pltpu.make_async_remote_copy(
                        src_ref=array.at[:, to(off), j], dst_ref=land.at[a, me, j],
                        send_sem=send_sem.at[a], recv_sem=recv_sem.at[a, me],
                        device_id={"head": to(off)}, device_id_type=MESH,
                    ).start()

    for ref in (k_high, k_low, v_high, v_low):

        def clear(s, _, ref=ref):
            for j in range(heads):
                ref[s, j, tokens:, :] = jnp.zeros((wide - tokens, wide), jnp.bfloat16)
            return 0

        lax.fori_loop(0, sources, clear, 0)
    ends = []
    for d in range(docs.shape[0]):
        ends.append(docs[d] + (ends[-1] if ends else 0))

    def doc_of(position):
        return sum((end <= position).astype(jnp.int32) for end in ends)

    row = lax.broadcasted_iota(jnp.int32, (tokens, wide), 0)
    col = lax.broadcasted_iota(jnp.int32, (tokens, wide), 1)
    upto_col = (row <= col).astype(jnp.float32)
    upto_row = (row >= col).astype(jnp.float32)[:, :tokens]

    def weigh(s, _):
        pltpu.make_async_copy(gate_in.at[s], gate_in.at[s], gate_recv.at[s]).wait()
        gate = gate_in[s]
        along_row = jnp.dot(gate, upto_col, precision=EXACT, preferred_element_type=jnp.float32)
        along_col = lax.dot_general(
            upto_row, gate, (((1,), (1,)), ((), ())), precision=EXACT, preferred_element_type=jnp.float32
        )
        start = (ctx * sources + s) * tokens
        doc_col = doc_of(start + row)
        doc_row = doc_of(start + col[:1])
        before = jnp.full((1, wide), start - 1, jnp.int32)
        doc_before = jnp.where(before >= 0, doc_of(before), -1)
        doc_last = doc_of(before + tokens)
        seen = (row >= col) & (doc_col == doc_row)
        same_first = doc_col == doc_before
        same_last = doc_col == doc_last
        for j in range(heads):
            col_sum = jnp.broadcast_to(along_col[:, j : j + 1], (tokens, wide))
            row_sum = along_row[j : j + 1, :]
            last = along_row[j : j + 1, tokens - 1 : tokens]
            keep[s, j] = jnp.exp(jnp.where(seen, col_sum - row_sum, BLOCKED))
            tail[s, j] = jnp.exp(jnp.where(same_last, last - col_sum, BLOCKED))
            through = jnp.exp(jnp.where(same_first, col_sum, BLOCKED))
            carry[s, j] = through
            step[s, j] = jnp.broadcast_to(through[tokens - 1 :, :], (8, wide))
        return 0

    lax.fori_loop(0, sources, weigh, 0)

    def arrived(a, s):
        pltpu.make_async_copy(land.at[a, s], land.at[a, s], recv_sem.at[a, s]).wait()

    filler = jnp.zeros((wide - tokens, wide), jnp.float32)

    def gather(n, _):
        s = source(n)
        arrived(K, s)
        arrived(V, s)
        for j in range(heads):
            keys = land[K, s, j]
            values = land[V, s, j]
            k_high[s, j, :tokens, :], k_low[s, j, :tokens, :] = split(keys)
            v_high[s, j, :tokens, :], v_low[s, j, :tokens, :] = split(values)
            weighted = jnp.concatenate([keys * tail[s, j], filler], axis=0)
            flipped = jnp.concatenate([values, filler], axis=0).T
            update[s, j] = product(
                jnp.concatenate(split(flipped), axis=1), twice(*split(weighted))
            )
        return 0

    lax.fori_loop(0, sources, gather, 0)

    for j in range(heads):

        def onward(s, running, j=j):
            state, factor = running
            return step[s, j, :1, :] * state + update[s, j], step[s, j] * factor

        state, factor = lax.fori_loop(
            0, sources, onward, (jnp.zeros((wide, wide), jnp.float32), jnp.ones((8, wide), jnp.float32))
        )
        own_state[j, :wide, :] = state
        own_state[j, wide:, :] = factor

    def pass_on(source_ref, target_ref, n, hop):
        return pltpu.make_async_remote_copy(
            src_ref=source_ref, dst_ref=target_ref, send_sem=state_send.at[n], recv_sem=state_recv.at[n],
            device_id={"ctx": (ctx + hop) % n_ctx}, device_id_type=MESH,
        )

    by_one = pass_on(own_state, near_states.at[0], 0, 1)
    by_two = pass_on(own_state, near_states.at[1], 1, 2)
    sums = pass_on(near_sum, far_sum, 2, 2)
    by_two.start()
    by_one.start()
    by_one.wait_recv()
    by_two.wait_recv()
    for j in range(heads):
        near_sum[j] = near_states[0, j, :wide, :] + near_states[0, j, wide : wide + 1, :] * near_states[1, j, :wide, :]
    sums.start()
    sums.wait_recv()

    for j in range(heads):
        both = near_states[0, j, wide : wide + 1, :] * near_states[1, j, wide : wide + 1, :]

        def enter(s, state, j=j):
            s_high[s, j], s_low[s, j] = split(state)
            return step[s, j, :1, :] * state + update[s, j]

        lax.fori_loop(0, sources, enter, near_sum[j] + both * far_sum[j])

    def answer(n, _):
        s = source(n)
        arrived(Q, s)
        for j in range(heads):
            queries = jnp.concatenate(split(land[Q, s, j]), axis=1)
            scores = product_t(queries, stacked(k_high[s, j], k_low[s, j]))
            carried = product_t(queries, stacked(s_high[s, j], s_low[s, j]))
            weights = jnp.concatenate(split(scores * keep[s, j]), axis=1)
            mixed = product(weights, twice(v_high[s, j], v_low[s, j])) + carry[s, j] * carried
            size = jnp.mean(mixed * mixed, axis=1, keepdims=True)
            rows_out[pl.ds(s * (tokens * heads) + j, tokens, stride=heads), :] = mixed * lax.rsqrt(size + EPSILON)
        pltpu.make_async_copy(
            rows_out.at[pl.ds(s * (tokens * heads), tokens * heads)].reshape(tokens, heads, wide),
            out.at[pl.ds(s * tokens, tokens)],
            out_sem,
        ).start()
        return 0

    lax.fori_loop(0, sources, answer, 0)

    by_one.wait_send()
    by_two.wait_send()
    sums.wait_send()
    others = pl.ds(0, sources - 1)
    pltpu.make_async_copy(gates.at[others], gates.at[others], gate_send).wait()
    for a, array in enumerate(arrays):
        pltpu.make_async_copy(array.at[:, others], array.at[:, others], send_sem.at[a]).wait()
    pltpu.make_async_copy(out, out, out_sem).wait()


def per_device(n_ctx, queries, key_vectors, value_vectors, log_decay, doc_lengths):
    tokens, sources, heads, wide = queries.shape
    f32 = jnp.float32
    hbm = pl.BlockSpec(memory_space=pl.ANY)
    per_block = (sources, heads)
    block = pltpu.VMEM((*per_block, tokens, wide), f32)
    square = pltpu.VMEM((*per_block, wide, wide), jnp.bfloat16)
    states = pltpu.VMEM((heads, wide, wide), f32)
    total = tokens * sources
    return pl.pallas_call(
        functools.partial(kernel, tokens, heads, n_ctx),
        out_shape=jax.ShapeDtypeStruct((total, heads, wide), f32),
        in_specs=[pl.BlockSpec(memory_space=pltpu.SMEM), hbm, hbm, hbm, hbm],
        out_specs=hbm,
        scratch_shapes=[
            pltpu.VMEM((3, *per_block, tokens, wide), f32),
            pltpu.VMEM((sources, heads, tokens), f32),
            block,
            block,
            block,
            pltpu.VMEM((*per_block, 8, wide), f32),
            pltpu.VMEM((*per_block, wide, wide), f32),
            *[square] * 6,
            pltpu.VMEM((heads, wide + 8, wide), f32),
            pltpu.VMEM((2, heads, wide + 8, wide), f32),
            states,
            states,
            pltpu.VMEM((total * heads, wide), f32),
            pltpu.SemaphoreType.DMA((3,)),
            pltpu.SemaphoreType.DMA((3, sources)),
            pltpu.SemaphoreType.DMA,
            pltpu.SemaphoreType.DMA((sources,)),
            pltpu.SemaphoreType.DMA((3,)),
            pltpu.SemaphoreType.DMA((3,)),
            pltpu.SemaphoreType.DMA,
        ],
        compiler_params=pltpu.CompilerParams(
            collective_id=0, has_side_effects=True, vmem_limit_bytes=56 << 20
        ),
        name="lightning",
    )(doc_lengths, queries, key_vectors, value_vectors, jnp.transpose(log_decay, (1, 2, 0)))


def solution(mesh):
    return jax.shard_map(
        functools.partial(per_device, mesh.shape["ctx"]),
        mesh=mesh,
        in_specs=(
            P(("ctx", "head"), None, None, None),
            P(("ctx", "head"), None, None, None),
            P(("ctx", "head"), None, None, None),
            P(("ctx", "head"), None, None),
            P(),
        ),
        out_specs=P("ctx", "head", None),
        check_vma=False,
    )
```

time: 445 us -> 122 us (0.27)
  the two profiles are of different devices: /device:TPU:128 before, /device:TPU:10 now
where the time goes in v1:
time: 122 us
  Pallas kernels  119 us (98%)
  local copies, waits for them, and re-layouts  3.18 us (3%)
    pallas_call x1, Pallas kernels, per_device(): pl.pallas_call(functools.partial(kernel, tokens, heads, n_ctx), out_shape...  119 us
    unnamed x1, local copies, waits for them, and re-layouts  3.18 us

profile of v1, /device:TPU:10, one launch (start us, length us, event | category | flops | bytes accessed | tf_op | source)
XLA Modules:
  0.0 121.8 jit_solution(5069180554256546757)
XLA Ops:
  0.0 118.6 %lightning.1 = f32[1536,4,128]{2,1,0:T(4,128)} custom-call(s32[16]{0:T(128)} %docs.1, f32[96,16,4,128]{3,2,1,0:T(4,128)} %q.1, f32[96,16,4,128]{3,2,1,0:T(4,128)} %k.1, f32[96,16,4,128]{3,2,1,0:T(4,128)} %v.1, f32[16,4,96]{2,1,0:T(4,128)} %bitcast.1), custom_call_target="tpu_custom_call" | custom-call | tf_op jit(solution)/shard_map/lightning/pallas_call | solution.py:262
  118.6 3.2 %copy.7 = f32[1536,4,128]{2,1,0:T(4,128)} copy(f32[1536,4,128]{2,1,0:T(4,128)} %lightning.1) | data formatting | bytes 6291456

commit v2 on v1

v2 whole, which is shorter than its diff:
```python
import functools

import jax
import jax.numpy as jnp
from jax import lax
from jax.experimental import pallas as pl
from jax.experimental.pallas import tpu as pltpu
from jax.sharding import PartitionSpec as P

EPSILON = 1e-06
SIDE = 4
BLOCKED = -1e30
EXACT = lax.Precision.HIGHEST
MESH = pl.DeviceIdType.MESH

MIXED = (10, 1, 6, 3, 9, 4, 14, 12, 11, 5, 2, 15, 8, 7, 13)
GROUPS = ((1, 3, 4, 12), (5, 15, 7, 13), (2, 8), (6, 14, 9, 11), (10,))
USED = (0,) + sum(GROUPS, ())


def packed(offsets):
    code = sum(off << (4 * n) for n, off in enumerate(offsets))
    return code - (1 << 32) if code >= 1 << 31 else code


FIRST_CODES, LAST_CODES = packed(USED[:8]), packed(USED[8:])


def split(x):
    high = x.astype(jnp.bfloat16)
    return high, (x - high.astype(jnp.float32)).astype(jnp.bfloat16)


def twice(high, low):
    row = jnp.concatenate([high, low], axis=1)
    return jnp.concatenate([row, row], axis=0)


def stacked(high, low):
    return jnp.concatenate(
        [jnp.concatenate([high, high], axis=1), jnp.concatenate([low, low], axis=1)],
        axis=0,
    )


def halves(x):
    half = x.shape[1] // 2
    return x[:, :half] + x[:, half:]


def product(left, right):
    return halves(jnp.dot(left, right, preferred_element_type=jnp.float32))


def product_t(left, right):
    return halves(
        lax.dot_general(
            left, right, (((1,), (1,)), ((), ())), preferred_element_type=jnp.float32
        )
    )


def kernel(
    tokens, heads, n_ctx,
    docs_in, q, k, v, gates, out,
    land_kv, land_q, gate_in, keep, tail, carry, step, update,
    k_high, k_low, v_high, v_low, s_high, s_low, own_state, near_states, near_sum, far_sum, docs, docs_sem,
    kv_send, kv_recv, q_send, q_recv, gate_send, gate_recv, state_send, state_recv,
):
    sources = SIDE * SIDE
    wide = 128
    ctx = lax.axis_index("ctx")
    me = lax.axis_index("head")
    x, y = me // SIDE, me % SIDE

    def to(off):
        return (x + off // SIDE) % SIDE * SIDE + (y + off % SIDE) % SIDE

    def source(n):
        codes = jnp.where(n < 8, FIRST_CODES, LAST_CODES)
        off = lax.shift_right_arithmetic(codes, 4 * (n % 8)) % 16
        return (x + SIDE - off // SIDE) % SIDE * SIDE + (y + SIDE - off % SIDE) % SIDE

    pltpu.make_async_copy(docs_in, docs, docs_sem).start()
    for j in range(heads):
        for a, array in enumerate((k, v)):
            pltpu.make_async_copy(
                array.at[:, me, j], land_kv.at[j, me, a], kv_recv.at[j, me]
            ).start()
        pltpu.make_async_copy(q.at[:, me, j], land_q.at[j, me], q_recv.at[j, me]).start()
    pltpu.make_async_copy(gates.at[me], gate_in.at[me], gate_recv.at[me]).start()

    barrier = pltpu.get_barrier_semaphore()
    for off in range(1, sources):
        pl.semaphore_signal(barrier, inc=1, device_id={"head": to(off)}, device_id_type=MESH)
    for hop in (1, 2, n_ctx - 1, n_ctx - 2):
        pl.semaphore_signal(
            barrier, inc=1, device_id={"ctx": (ctx + hop) % n_ctx}, device_id_type=MESH
        )
    pl.semaphore_wait(barrier, sources + 3)

    def send(source_ref, target_ref, send_sem, recv_sem, off):
        pltpu.make_async_remote_copy(
            src_ref=source_ref, dst_ref=target_ref, send_sem=send_sem, recv_sem=recv_sem,
            device_id={"head": to(off)}, device_id_type=MESH,
        ).start()

    for off in MIXED:
        send(gates.at[to(off)], gate_in.at[me], gate_send, gate_recv.at[me], off)
    for a, array in enumerate((k, v)):
        for j in range(heads):
            for off in MIXED:
                send(array.at[:, to(off), j], land_kv.at[j, me, a], kv_send.at[a], kv_recv.at[j, me], off)
    for group in GROUPS:
        for j in range(heads):
            for off in group:
                send(q.at[:, to(off), j], land_q.at[j, me], q_send, q_recv.at[j, me], off)

    for ref in (k_high, k_low, v_high, v_low):

        def clear(s, _, ref=ref):
            for j in range(heads):
                ref[j, s, tokens:, :] = jnp.zeros((wide - tokens, wide), jnp.bfloat16)
            return 0

        lax.fori_loop(0, sources, clear, 0)
    pltpu.make_async_copy(docs_in, docs, docs_sem).wait()
    ends = []
    for d in range(docs.shape[0]):
        ends.append(docs[d] + (ends[-1] if ends else 0))

    def doc_of(position):
        return sum((end <= position).astype(jnp.int32) for end in ends)

    row = lax.broadcasted_iota(jnp.int32, (tokens, wide), 0)
    col = lax.broadcasted_iota(jnp.int32, (tokens, wide), 1)
    upto_col = (row <= col).astype(jnp.float32)
    upto_row = (row >= col).astype(jnp.float32)[:, :tokens]

    def weigh(s, _):
        pltpu.make_async_copy(gate_in.at[s], gate_in.at[s], gate_recv.at[s]).wait()
        gate = gate_in[s]
        along_row = jnp.dot(gate, upto_col, precision=EXACT, preferred_element_type=jnp.float32)
        along_col = lax.dot_general(
            upto_row, gate, (((1,), (1,)), ((), ())), precision=EXACT, preferred_element_type=jnp.float32
        )
        start = (ctx * sources + s) * tokens
        doc_col = doc_of(start + row)
        doc_row = doc_of(start + col[:1])
        before = jnp.full((1, wide), start - 1, jnp.int32)
        doc_before = jnp.where(before >= 0, doc_of(before), -1)
        doc_last = doc_of(before + tokens)
        seen = (row >= col) & (doc_col == doc_row)
        same_first = doc_col == doc_before
        same_last = doc_col == doc_last
        for j in range(heads):
            col_sum = jnp.broadcast_to(along_col[:, j : j + 1], (tokens, wide))
            row_sum = along_row[j : j + 1, :]
            last = along_row[j : j + 1, tokens - 1 : tokens]
            keep[j, s] = jnp.exp(jnp.where(seen, col_sum - row_sum, BLOCKED))
            tail[j, s] = jnp.exp(jnp.where(same_last, last - col_sum, BLOCKED))
            through = jnp.exp(jnp.where(same_first, col_sum, BLOCKED))
            carry[j, s] = through
            step[j, s] = jnp.broadcast_to(through[tokens - 1 :, :], (8, wide))
        return 0

    lax.fori_loop(0, sources, weigh, 0)

    filler = jnp.zeros((wide - tokens, wide), jnp.float32)

    def gather(j, s):
        keys = land_kv[j, s, 0]
        values = land_kv[j, s, 1]
        k_high[j, s, :tokens, :], k_low[j, s, :tokens, :] = split(keys)
        v_high[j, s, :tokens, :], v_low[j, s, :tokens, :] = split(values)
        weighted = jnp.concatenate([keys * tail[j, s], filler], axis=0)
        flipped = jnp.concatenate([values, filler], axis=0).T
        update[j, s] = product(
            jnp.concatenate(split(flipped), axis=1), twice(*split(weighted))
        )

    def hand_on(source_ref, target_ref, n, j, hop):
        return pltpu.make_async_remote_copy(
            src_ref=source_ref.at[j], dst_ref=target_ref.at[j],
            send_sem=state_send.at[n, j], recv_sem=state_recv.at[n, j],
            device_id={"ctx": (ctx + hop) % n_ctx}, device_id_type=MESH,
        )

    def by_one(j):
        return hand_on(own_state, near_states.at[0], 0, j, 1)

    def by_two(j):
        return hand_on(own_state, near_states.at[1], 1, j, 2)

    def sums(j):
        return hand_on(near_sum, far_sum, 2, j, 2)

    def close(j):
        def onward(s, running):
            state, factor = running
            return step[j, s, :1, :] * state + update[j, s], step[j, s] * factor

        state, factor = lax.fori_loop(
            0, sources, onward, (jnp.zeros((wide, wide), jnp.float32), jnp.ones((8, wide), jnp.float32))
        )
        own_state[j, :wide, :] = state
        own_state[j, wide:, :] = factor
        by_two(j).start()
        by_one(j).start()

    def join(j):
        by_one(j).wait_recv()
        by_two(j).wait_recv()
        near_sum[j] = near_states[0, j, :wide, :] + near_states[0, j, wide : wide + 1, :] * near_states[1, j, :wide, :]
        sums(j).start()

    def enter(j):
        sums(j).wait_recv()
        both = near_states[0, j, wide : wide + 1, :] * near_states[1, j, wide : wide + 1, :]

        def onward(s, state):
            s_high[j, s], s_low[j, s] = split(state)
            return step[j, s, :1, :] * state + update[j, s]

        lax.fori_loop(0, sources, onward, near_sum[j] + both * far_sum[j])

    rows_out = out.reshape(sources * tokens * heads, wide)

    def answer(j, s):
        queries = jnp.concatenate(split(land_q[j, s]), axis=1)
        scores = product_t(queries, stacked(k_high[j, s], k_low[j, s]))
        carried = product_t(queries, stacked(s_high[j, s], s_low[j, s]))
        weights = jnp.concatenate(split(scores * keep[j, s]), axis=1)
        mixed = product(weights, twice(v_high[j, s], v_low[j, s])) + carry[j, s] * carried
        size = jnp.mean(mixed * mixed, axis=1, keepdims=True)
        rows_out[pl.ds(s * (tokens * heads) + j, tokens, stride=heads), :] = mixed * lax.rsqrt(size + EPSILON)

    def over_sources(work, land, recv_sem):
        def one(n, _):
            s = source(n)
            for j in range(heads):
                pltpu.make_async_copy(land.at[j, s], land.at[j, s], recv_sem.at[j, s]).wait()
            for j in range(heads):
                work(j, s)
            return 0

        lax.fori_loop(0, sources, one, 0)

    over_sources(gather, land_kv, kv_recv)
    for j in range(heads):
        close(j)
    for j in range(heads):
        join(j)
    for j in range(heads):
        enter(j)
    over_sources(answer, land_q, q_recv)

    for j in range(heads):
        by_one(j).wait_send()
        by_two(j).wait_send()
        sums(j).wait_send()
    others = pl.ds(0, sources - 1)
    pltpu.make_async_copy(gates.at[others], gates.at[others], gate_send).wait()
    for array, sem in ((k, kv_send.at[0]), (v, kv_send.at[1]), (q, q_send)):
        pltpu.make_async_copy(array.at[:, others], array.at[:, others], sem).wait()


def per_device(n_ctx, queries, key_vectors, value_vectors, log_decay, doc_lengths):
    tokens, sources, heads, wide = queries.shape
    f32 = jnp.float32
    hbm = pl.BlockSpec(memory_space=pltpu.HBM)
    per_block = (heads, sources)
    block = pltpu.VMEM((*per_block, tokens, wide), f32)
    square = pltpu.VMEM((*per_block, wide, wide), jnp.bfloat16)
    states = pltpu.VMEM((heads, wide, wide), f32)
    dma = pltpu.SemaphoreType.DMA

    def stays(array):
        return pltpu.with_memory_space_constraint(array, pltpu.HBM)

    return pl.pallas_call(
        functools.partial(kernel, tokens, heads, n_ctx),
        out_shape=jax.ShapeDtypeStruct((sources * tokens, heads, wide), f32),
        in_specs=[hbm] * 5,
        out_specs=pl.BlockSpec(memory_space=pltpu.VMEM),
        scratch_shapes=[
            pltpu.VMEM((*per_block, 2, tokens, wide), f32),
            block,
            pltpu.VMEM((sources, heads, tokens), f32),
            block,
            block,
            block,
            pltpu.VMEM((*per_block, 8, wide), f32),
            pltpu.VMEM((*per_block, wide, wide), f32),
            *[square] * 6,
            pltpu.VMEM((heads, wide + 8, wide), f32),
            pltpu.VMEM((2, heads, wide + 8, wide), f32),
            states,
            states,
            pltpu.SMEM(doc_lengths.shape, jnp.int32),
            dma,
            dma((2,)),
            dma(per_block),
            dma,
            dma(per_block),
            dma,
            dma((sources,)),
            dma((3, heads)),
            dma((3, heads)),
        ],
        compiler_params=pltpu.CompilerParams(
            collective_id=0, has_side_effects=True, vmem_limit_bytes=48 << 20
        ),
        name="lightning",
    )(
        stays(doc_lengths), queries, key_vectors, value_vectors, stays(jnp.transpose(log_decay, (1, 2, 0)))
    )


def solution(mesh):
    return jax.shard_map(
        functools.partial(per_device, mesh.shape["ctx"]),
        mesh=mesh,
        in_specs=(
            P(("ctx", "head"), None, None, None),
            P(("ctx", "head"), None, None, None),
            P(("ctx", "head"), None, None, None),
            P(("ctx", "head"), None, None),
            P(),
        ),
        out_specs=P("ctx", "head", None),
        check_vma=False,
    )
```

time: 122 us -> 118 us (0.967); the launches traced: 122 us -> 116 us
  Pallas kernels: 119 us -> 115 us
  local copies, waits for them, and re-layouts: 3.18 us -> 1.67 us
    pallas_call x1, Pallas kernels: 119 us -> 115 us  [per_device(): pl.pallas_call(functools.partial(kernel, tokens, heads, n_ctx), out_shape...]
    unnamed x1, local copies, waits for them, and re-layouts: 3.18 us -> 1.67 us
where the time goes in v2:
time: 118 us; the launch traced here: 116 us
  Pallas kernels  115 us (97%)
  local copies, waits for them, and re-layouts  1.67 us (1%)
    pallas_call x1, Pallas kernels, per_device(): pl.pallas_call(functools.partial(kernel, tokens, heads, n_ctx), out_shape...  115 us

profile of v2, /device:TPU:10, one launch (start us, length us, event | category | flops | bytes accessed | tf_op | source)
XLA Modules:
  0.0 116.5 jit_solution(1166823592421752800)
XLA Ops:
  0.0 114.8 %lightning.1 = f32[1536,4,128]{2,1,0:T(4,128)S(1)} custom-call(s32[16]{0:T(128)} %docs_in.1, f32[96,16,4,128]{3,2,1,0:T(4,128)} %q.1, f32[96,16,4,128]{3,2,1,0:T(4,128)} %k.1, f32[96,16,4,128]{3,2,1,0:T(4,128)} %v.1, f32[16,4,96]{2,1,0:T(4,128)} %bitcast.1), custom_call_target="tpu_custom_call" | custom-call | tf_op jit(solution)/shard_map/lightning/pallas_call | solution.py:281
  114.8 1.7 %copy.7 = f32[1536,4,128]{2,1,0:T(4,128)} copy(f32[1536,4,128]{2,1,0:T(4,128)S(1)} %lightning.1) | data formatting | bytes 6291456

commit v3 on v2

--- a/solution.py
+++ b/solution.py
@@ -73,14 +73,25 @@
     me = lax.axis_index("head")
     x, y = me // SIDE, me % SIDE
 
+    rows_of = [(x + d) % SIDE * SIDE for d in range(SIDE)]
+    columns_of = [(y + d) % SIDE for d in range(SIDE)]
+    places = [a + b for a in rows_of for b in columns_of]
+
     def to(off):
-        return (x + off // SIDE) % SIDE * SIDE + (y + off % SIDE) % SIDE
+        return places[off]
 
     def source(n):
         codes = jnp.where(n < 8, FIRST_CODES, LAST_CODES)
         off = lax.shift_right_arithmetic(codes, 4 * (n % 8)) % 16
         return (x + SIDE - off // SIDE) % SIDE * SIDE + (y + SIDE - off % SIDE) % SIDE
 
+    barrier = pltpu.get_barrier_semaphore()
+    for off in range(1, sources):
+        pl.semaphore_signal(barrier, inc=1, device_id={"head": to(off)}, device_id_type=MESH)
+    for hop in (1, 2, n_ctx - 1, n_ctx - 2):
+        pl.semaphore_signal(
+            barrier, inc=1, device_id={"ctx": (ctx + hop) % n_ctx}, device_id_type=MESH
+        )
     pltpu.make_async_copy(docs_in, docs, docs_sem).start()
     for j in range(heads):
         for a, array in enumerate((k, v)):
@@ -90,13 +101,6 @@
         pltpu.make_async_copy(q.at[:, me, j], land_q.at[j, me], q_recv.at[j, me]).start()
     pltpu.make_async_copy(gates.at[me], gate_in.at[me], gate_recv.at[me]).start()
 
-    barrier = pltpu.get_barrier_semaphore()
-    for off in range(1, sources):
-        pl.semaphore_signal(barrier, inc=1, device_id={"head": to(off)}, device_id_type=MESH)
-    for hop in (1, 2, n_ctx - 1, n_ctx - 2):
-        pl.semaphore_signal(
-            barrier, inc=1, device_id={"ctx": (ctx + hop) % n_ctx}, device_id_type=MESH
-        )
     pl.semaphore_wait(barrier, sources + 3)
 
     def send(source_ref, target_ref, send_sem, recv_sem, off):
@@ -105,12 +109,12 @@
             device_id={"head": to(off)}, device_id_type=MESH,
         ).start()
 
-    for off in MIXED:
-        send(gates.at[to(off)], gate_in.at[me], gate_send, gate_recv.at[me], off)
     for a, array in enumerate((k, v)):
         for j in range(heads):
             for off in MIXED:
                 send(array.at[:, to(off), j], land_kv.at[j, me, a], kv_send.at[a], kv_recv.at[j, me], off)
+                if j == a == 0:
+                    send(gates.at[to(off)], gate_in.at[me], gate_send, gate_recv.at[me], off)
     for group in GROUPS:
         for j in range(heads):
             for off in group:

time: 118 us -> 118 us (level)
  no operation moved by 1% of the time
where the time goes in v3:
time: 118 us; the launch traced here: 117 us
  Pallas kernels  115 us (97%)
  local copies, waits for them, and re-layouts  1.67 us (1%)
    pallas_call x1, Pallas kernels, per_device(): pl.pallas_call(functools.partial(kernel, tokens, heads, n_ctx), out_shape...  115 us

profile of v3, /device:TPU:10, one launch (start us, length us, event | category | flops | bytes accessed | tf_op | source)
XLA Modules:
  0.0 116.9 jit_solution(15396618457015335102)
XLA Ops:
  0.0 115.2 %lightning.1 = f32[1536,4,128]{2,1,0:T(4,128)S(1)} custom-call(s32[16]{0:T(128)} %docs_in.1, f32[96,16,4,128]{3,2,1,0:T(4,128)} %q.1, f32[96,16,4,128]{3,2,1,0:T(4,128)} %k.1, f32[96,16,4,128]{3,2,1,0:T(4,128)} %v.1, f32[16,4,96]{2,1,0:T(4,128)} %bitcast.1), custom_call_target="tpu_custom_call" | custom-call | tf_op jit(solution)/shard_map/lightning/pallas_call | solution.py:285
  115.2 1.7 %copy.7 = f32[1536,4,128]{2,1,0:T(4,128)} copy(f32[1536,4,128]{2,1,0:T(4,128)S(1)} %lightning.1) | data formatting | bytes 6291456
